TPU v7x, 128 devices: a whole 4x4x4 slice. The times are simulated.
128 devices in a mesh: row: 8 (over x, z_hi), col: 16 (over z_lo, y, core).
Axes of the slice: x: 4, y: 4, z: 4 (z_hi: 2, z_lo: 2; z = z_hi * 2 + z_lo), core: 2. Of those that a mesh axis runs over, the one named last changes fastest.
Arguments:
- pair_state: bfloat16 [768, 768, 128], P(('row', 'col')), may hold values from -6 to 6
- single_rep: bfloat16 [16, 768, 768], P(None, ('row', 'col')), may hold values from -64 to 64
- token_mask: int32 [768], replicated, may hold values 0 or 1
- chain_ids: int32 [768], replicated, may hold values from 0 to 3, never falling along the last dimension, each value on 1 to 384 neighbouring positions
- pair_gain: float32 [128], replicated, may hold values from 0.1 to 1.9
- mix_gain: float32 [128], replicated, may hold values from 0.1 to 1.9
- left_weight: bfloat16 [128, 256], replicated, may hold values from -0.5 to 0.5
- right_weight: bfloat16 [128, 256], replicated, may hold values from -0.5 to 0.5
- gate_weight: bfloat16 [128, 128], replicated, may hold values from -0.5 to 0.5
- out_weight: bfloat16 [128, 128], replicated, may hold values from -0.5 to 0.5
- bias_weight: bfloat16 [128, 16], replicated, may hold values from -1.5 to 1.5
- token_weight: bfloat16 [768, 2304], replicated, may hold values from -0.21875 to 0.21875
- merge_weight: bfloat16 [768, 768], replicated, may hold values from -0.625 to 0.625
Outputs:
- pair_tiles: bfloat16 [768, 8, 16, 6, 128], P('row', None, 'col')
- attention_out: bfloat16 [16, 768, 768], P(None, ('row', 'col'))
Inputs may be any that keep to these rules, and one draw needn't show every extreme that they name: chain_ids never falls along the tokens; a chain holds 1 to 384 tokens.
All inputs are finite; a program needn't handle non-finite values.
Results may differ from a plain program's by a relative error of at most 0.034.
Values may be sent and summed in bfloat16 or wider, within the bound.
A program may use at most 256 MiB of HBM per device.

v0:
```python
import math

import jax
import jax.numpy as jnp
from jax import lax
from jax.sharding import PartitionSpec as P

epsilon = 1e-05


def normalize(values, norm_gain):
    floats = values.astype(jnp.float32)
    centered = floats - jnp.mean(floats, axis=-1, keepdims=True)
    variance = jnp.mean(centered * centered, axis=-1, keepdims=True)
    scaled = centered * lax.rsqrt(variance + epsilon)
    if norm_gain is None:
        return scaled
    return scaled * norm_gain


def gated_branch(normed, weight, pair_mask):
    half_width = weight.shape[0]
    hidden = jnp.einsum("ikc,ce->ike", normed, weight, preferred_element_type=jnp.float32)
    return (
        jax.nn.sigmoid(hidden[..., :half_width]) * hidden[..., half_width:] * pair_mask[..., None]
    ).astype(jnp.bfloat16)


def rows_blocks(pair_rows, valid_rows, valid_all, pair_gain, left_weight, group_count, group_rows):
    token_count = pair_rows.shape[1]
    channels = pair_rows.shape[2]

    def one_group(inputs):
        pair_group, valid_group = inputs
        normed_group = normalize(pair_group, pair_gain).astype(jnp.bfloat16)
        left_group = gated_branch(
            normed_group, left_weight, valid_group[:, None] * valid_all[None, :]
        )
        return (normed_group, left_group)

    grouped = (
        pair_rows.reshape(group_count, group_rows, token_count, channels),
        valid_rows.reshape(group_count, group_rows),
    )
    normed_groups, left_groups = lax.map(one_group, grouped)
    return (
        normed_groups.reshape(group_count * group_rows, token_count, channels),
        left_groups.reshape(group_count * group_rows, token_count, channels),
    )


def shards(
    pair_state,
    single_rep,
    token_mask,
    chain_ids,
    pair_gain,
    mix_gain,
    left_weight,
    right_weight,
    gate_weight,
    out_weight,
    bias_weight,
    token_weight,
    merge_weight,
):
    row_count = lax.axis_size("row")
    col_count = lax.axis_size("col")
    row_index = lax.axis_index("row")
    col_index = lax.axis_index("col")
    flat_rows = pair_state.shape[0]
    channels = pair_state.shape[2]
    samples = single_rep.shape[0]
    model_width = single_rep.shape[2]
    head_count = bias_weight.shape[1]
    head_width = model_width // head_count
    block_rows = flat_rows * col_count
    block_cols = flat_rows * row_count
    valid_all = (token_mask == 1).astype(jnp.float32)
    own_start = (row_index * col_count + col_index) * flat_rows
    row_start = row_index * block_rows
    valid_own = lax.dynamic_slice_in_dim(valid_all, own_start, flat_rows)
    valid_rows = lax.dynamic_slice_in_dim(valid_all, row_start, block_rows)
    valid_cols = lax.dynamic_index_in_dim(
        valid_all.reshape(row_count, col_count, flat_rows), col_index, 1, False
    ).reshape(block_cols)
    chain_rows = lax.dynamic_slice_in_dim(chain_ids, row_start, block_rows)
    chain_cols = lax.dynamic_index_in_dim(
        chain_ids.reshape(row_count, col_count, flat_rows), col_index, 1, False
    ).reshape(block_cols)
    projected = jnp.einsum(
        "std,de->ste", single_rep, token_weight, preferred_element_type=jnp.float32
    ).astype(jnp.bfloat16)
    queries = projected[..., :model_width]
    keys_own = projected[..., model_width : 2 * model_width]
    values_own = projected[..., 2 * model_width :]
    normed_own = normalize(pair_state, pair_gain).astype(jnp.bfloat16)
    own_mask = valid_own[:, None] * valid_all[None, :]
    right_own = gated_branch(normed_own, right_weight, own_mask)
    right_cols, keys_cols, values_cols = (
        lax.all_gather(right_own, "row", axis=0, tiled=True),
        lax.all_gather(keys_own, "row", axis=1, tiled=True),
        lax.all_gather(values_own, "row", axis=1, tiled=True),
    )
    pair_rows, query_rows = (
        lax.all_gather(pair_state, "col", axis=0, tiled=True),
        lax.all_gather(queries, "col", axis=1, tiled=True),
    )
    normed_rows, left_rows = rows_blocks(
        pair_rows, valid_rows, valid_all, pair_gain, left_weight, col_count, flat_rows
    )
    pair_tile = lax.dynamic_index_in_dim(
        pair_rows.reshape(block_rows, row_count, col_count, flat_rows, channels),
        col_index,
        2,
        False,
    ).reshape(block_rows, block_cols, channels)
    normed_tile = lax.dynamic_index_in_dim(
        normed_rows.reshape(block_rows, row_count, col_count, flat_rows, channels),
        col_index,
        2,
        False,
    ).reshape(block_rows, block_cols, channels)
    mixed_pairs = jnp.einsum(
        "ikc,jkc->ijc", left_rows, right_cols, preferred_element_type=jnp.float32
    )
    mixed_norm = normalize(mixed_pairs, mix_gain).astype(jnp.bfloat16)
    gate_value = jax.nn.sigmoid(
        jnp.einsum("ijc,ce->ije", normed_tile, gate_weight, preferred_element_type=jnp.float32)
    )
    update = jnp.einsum("ijc,ce->ije", mixed_norm, out_weight, preferred_element_type=jnp.float32)
    pair_new = (pair_tile.astype(jnp.float32) + gate_value * update).astype(jnp.bfloat16)
    bias_input = normalize(pair_new, None).astype(jnp.bfloat16)
    pair_bias = jnp.einsum(
        "ijc,ch->hij", bias_input, bias_weight, preferred_element_type=jnp.float32
    )
    query_heads = query_rows.reshape(samples, block_rows, head_count, head_width)
    key_heads = keys_cols.reshape(samples, block_cols, head_count, head_width)
    value_heads = values_cols.reshape(samples, block_cols, head_count, head_width)
    score_scale = 1.0 / math.sqrt(head_width)
    scores = (
        jnp.einsum("sihd,sjhd->shij", query_heads, key_heads, preferred_element_type=jnp.float32)
        * score_scale
        + pair_bias[None]
    )
    row_ids = row_start + jnp.arange(block_rows, dtype=jnp.int32)
    col_ids = (
        (jnp.arange(row_count, dtype=jnp.int32)[:, None] * col_count + col_index) * flat_rows
        + jnp.arange(flat_rows, dtype=jnp.int32)[None, :]
    ).reshape(block_cols)
    allowed = (valid_cols[None, :] > 0.5) & (chain_rows[:, None] == chain_cols[None, :]) | (
        row_ids[:, None] == col_ids[None, :]
    )
    local_max = jnp.max(jnp.where(allowed[None, None], scores, -1e30), axis=-1)
    row_max = lax.pmax(local_max.astype(jnp.bfloat16), "col").astype(local_max.dtype)
    weights = jnp.where(allowed[None, None], jnp.exp(scores - row_max[..., None]), 0.0).astype(
        jnp.bfloat16
    )
    totals = jnp.sum(weights.astype(jnp.float32), axis=-1)
    summed = jnp.einsum(
        "shij,sjhd->sihd", weights, value_heads, preferred_element_type=jnp.float32
    ).reshape(samples, block_rows, model_width)
    summed_own, totals_own = (
        lax.psum_scatter(
            summed.astype(jnp.bfloat16), "col", scatter_dimension=1, tiled=True
        ).astype(jnp.float32),
        lax.psum_scatter(
            totals.astype(jnp.bfloat16), "col", scatter_dimension=2, tiled=True
        ).astype(jnp.float32),
    )
    attended = (
        summed_own.reshape(samples, flat_rows, head_count, head_width)
        / jnp.transpose(totals_own, (0, 2, 1))[..., None]
    ).astype(jnp.bfloat16)
    attended = attended.reshape(samples, flat_rows, model_width)
    attention_out = jnp.einsum(
        "std,de->ste", attended, merge_weight, preferred_element_type=jnp.float32
    ).astype(jnp.bfloat16)
    return (pair_new.reshape(block_rows, row_count, 1, flat_rows, channels), attention_out)


def solution(mesh):
    in_specs = (
        P(("row", "col"), None, None),
        P(None, ("row", "col"), None),
        P(),
        P(),
        P(),
        P(),
        P(),
        P(),
        P(),
        P(),
        P(),
        P(),
        P(),
    )
    out_specs = (P("row", None, "col", None, None), P(None, ("row", "col"), None))
    return jax.shard_map(shards, mesh=mesh, in_specs=in_specs, out_specs=out_specs, check_vma=False)
```

profile of v0, /device:TPU:1, one launch (start us, length us, event | category | flops | bytes accessed | tf_op | source)
XLA Modules:
  0.0 883.4 jit_solution(9428254966866073664)
XLA Ops:
  21.4 40.4 %all-gather.14.cloned.1.call-done = bf16[16,48,768]{2,0,1:T(8,128)(2,1)} async-done(((bf16[16,6,768]{2,0,1:T(8,128)(2,1)}), bf16[16,48,768]{2,0,1:T(8,128)(2,1)}) %all-gather.14.cloned.1.call-update) | async-done | bytes 1179664 | tf_op jit(solution)/shard_map/all_gather | solution.py:102
  61.8 5.7 reshape.290
  67.6 44.2 %all-gather.10.cloned.1.call-done = bf16[16,48,768]{2,0,1:T(8,128)(2,1)} async-done(((bf16[16,6,768]{2,0,1:T(8,128)(2,1)}), bf16[16,48,768]{2,0,1:T(8,128)(2,1)}) %all-gather.10.cloned.1.call-update) | async-done | bytes 1179664 | tf_op jit(solution)/shard_map/all_gather | solution.py:103
  111.7 4.2 copy.104
  116.0 32.6 %all-gather.12.cloned.1.call-done = bf16[16,96,768]{2,0,1:T(8,128)(2,1)} async-done(((bf16[16,6,768]{2,0,1:T(8,128)(2,1)}), bf16[16,96,768]{2,0,1:T(8,128)(2,1)}) %all-gather.12.cloned.1.call-update) | async-done | bytes 2359312 | tf_op jit(solution)/shard_map/all_gather | solution.py:107
  148.5 4.6 copy.105
  153.2 116.0 %all-gather.8.cloned.1.call-done = bf16[48,768,128]{2,1,0:T(8,128)(2,1)} async-done(((bf16[6,768,128]{2,1,0:T(8,128)(2,1)}), bf16[48,768,128]{2,1,0:T(8,128)(2,1)}) %all-gather.8.cloned.1.call-update) | async-done | bytes 9437200 | tf_op jit(solution)/shard_map/all_gather | solution.py:101
  269.1 13.0 %copy.99 = bf16[48,768,128]{1,0,2:T(8,128)(2,1)} copy(bf16[48,768,128]{2,1,0:T(8,128)(2,1)} %all-gather.8.cloned.1.call-done) | data formatting | bytes 18874368 | tf_op jit(solution)/shard_map/all_gather | solution.py:101
  282.1 88.7 %all-gather.6.cloned.1.call-done = bf16[96,768,128]{2,1,0:T(8,128)(2,1)} async-done(((bf16[6,768,128]{2,1,0:T(8,128)(2,1)}), bf16[96,768,128]{2,1,0:T(8,128)(2,1)}) %all-gather.6.cloned.1.call-update) | async-done | bytes 18874384 | tf_op jit(solution)/shard_map/all_gather | solution.py:106
  370.8 212.1 %while.12 = (s32[]{:T(128)}, bf16[16,6,768,128]{3,2,1,0:T(8,128)(2,1)}, bf16[16,6,768,128]{3,2,1,0:T(8,128)(2,1)}, bf16[16,6,768,128]{3,2,1,0:T(8,128)(2,1)}, f3...) while((s32[]{:T(128)}, ...), condition=%wide.region_3.4_spmd, body=%wide.region_0.0_spmd.sunk | while | flops 314975232 | bytes 16826032 | solution.py:45
  375.0 3.5 fusion.84
  380.2 3.9 fusion.82
  388.3 3.5 fusion.84
  393.5 3.9 fusion.82
  406.8 3.8 fusion.82
  414.8 3.5 fusion.84
  420.0 3.9 fusion.82
  433.3 3.8 fusion.82
  446.6 3.8 fusion.82
  454.6 3.5 fusion.84
  459.8 3.9 fusion.82
  473.0 3.8 fusion.82
  481.1 3.5 fusion.84
  486.3 3.9 fusion.82
  494.4 3.5 fusion.84
  499.6 3.8 fusion.82
  507.6 3.5 fusion.84
  512.8 3.8 fusion.82
  520.8 3.5 fusion.84
  526.1 3.8 fusion.82
  539.3 3.8 fusion.82
  547.4 3.5 fusion.84
  552.6 3.9 fusion.82
  560.6 3.5 fusion.84
  565.8 3.8 fusion.82
  573.9 3.5 fusion.84
  579.1 3.9 fusion.82
  582.9 24.4 %copy.100 = bf16[96,768,128]{1,0,2:T(8,128)(2,1)} copy(bf16[96,768,128]{2,1,0:T(8,128)(2,1)} %bitcast.97) | data formatting | bytes 37748736 | tf_op jit(solution)/shard_map/reshape | solution.py:48
  607.3 12.4 %bitcast_reduce_fusion = (f32[96,48]{0,1:T(8,128)S(1)}, f32[128,48,96]{2,1,0:T(8,128)S(1)}) fusion(bf16[48,768,128]{1,0,2:T(8,128)(2,1)} %copy.99, bf16[96,768,128]{1,0,2:T(8,128)(2,1)} %copy.100), kind=kOutput, calls=%fused_computation.42 | convolution fusion | flops 906554880 | bytes 30689280 | tf_op jit(solution)/shard_map/ikc,jkc->ijc/dot_general | solution.py:124
  625.2 31.1 %reshape_reshape.3 = bf16[96,8,16,6,128]{4,3,2,1,0:T(8,128)(2,1)} reshape(bf16[16,6,768,128]{3,2,1,0:T(8,128)(2,1)} %get-tuple-element.45) | data formatting | bytes 37748736 | tf_op jit(solution)/shard_map/reshape;reshape | solution.py:119
  658.7 16.7 %copy.96 = bf16[96,768,128]{2,0,1:T(8,128)(2,1)S(1)} copy(bf16[96,768,128]{2,1,0:T(8,128)(2,1)} %bitcast.95) | data formatting | bytes 37748736 | tf_op jit(solution)/shard_map/all_gather | solution.py:106
  683.5 9.0 %select_reduce_fusion = (bf16[16,16,96]{2,1,0:T(8,128)(2,1)S(1)}, f32[16,16,96,48]{2,3,1,0:T(8,128)}) fusion(f32[16,96,48]{1,2,0:T(8,128)S(1)} %copy.112, pred[96,48]{0,1:T(8,128)(4,1)S(1)} %compare_or_fusion, bf16[16,96,16,48]{1,3,2,0:T(8,128)(2,1)} %bitcast.101, bf16[16,48,16,48]{3,2,0,1:T(8,128)(2,1)} %reshape.290), kind=kOutput, calls=%fused_computation.34 | convolution fusion | flops 117940224 | bytes 8606208 | tf_op jit(solution)/shard_map/sihd,sjhd->shij/dot_general | solution.py:142
  692.5 51.3 %pmax.7 = bf16[16,16,96]{2,1,0:T(8,128)(2,1)S(1)} all-reduce(bf16[16,16,96]{2,1,0:T(8,128)(2,1)S(1)} %get-tuple-element.90), channel_id=1, replica_groups=mesh['row'=8,'col'=16] {'col'}, use_global_device_ids=true, to_apply=%region_11.12 | all-reduce | flops 24576 | bytes 98304 | tf_op jit(solution)/shard_map/pmax | solution.py:155
  743.9 5.0 fusion.65
  750.3 7.2 convolution_convert_fusion
  757.5 4.9 copy.113
  764.5 44.8 %reduce-scatter.5.cloned.1.call-done = bf16[16,16,6]{1,0,2:T(8,128)(2,1)} async-done(((bf16[16,16,96]{1,0,2:T(8,128)(2,1)}), bf16[16,16,6]{1,0,2:T(8,128)(2,1)}) %reduce-scatter.5.cloned.1.call-update) | async-done | bytes 3088 | tf_op jit(solution)/shard_map/reduce_scatter | solution.py:167
  813.4 60.8 %reduce-scatter.3.cloned.1.call-done = bf16[16,6,768]{2,0,1:T(8,128)(2,1)} async-done(((bf16[16,96,768]{2,0,1:T(8,128)(2,1)}), bf16[16,6,768]{2,0,1:T(8,128)(2,1)}) %reduce-scatter.3.cloned.1.call-update) | async-done | bytes 147472 | tf_op jit(solution)/shard_map/reduce_scatter | solution.py:164
  (212 shorter events, 151.2 us)
Async XLA Ops:
  7.2 2.0 copy-start
  7.2 6.0 copy-start.9
  7.2 54.6 %all-gather.14.cloned.1.call-start = ((), (), s32[]{:S(2)}) async-start(), calls=%async_computation.6 | async-start | bytes 1327104 | tf_op jit(solution)/shard_map/all_gather | solution.py:102
  10.8 4.2 copy-start.2
  10.8 5.7 copy-start.5
  10.8 5.7 copy-start.6
  11.6 100.1 %all-gather.10.cloned.1.call-start = ((), (), s32[]{:S(2)}) async-start(), calls=%async_computation.4 | async-start | bytes 1327104 | tf_op jit(solution)/shard_map/all_gather | solution.py:103
  12.4 136.1 %all-gather.12.cloned.1.call-start = ((), (), s32[]{:S(2)}) async-start(), calls=%async_computation.5 | async-start | bytes 2506752 | tf_op jit(solution)/shard_map/all_gather | solution.py:107
  13.1 256.0 %all-gather.8.cloned.1.call-start = ((), (), s32[]{:S(2)}) async-start(), calls=%async_computation.3 | async-start | bytes 10616832 | tf_op jit(solution)/shard_map/all_gather | solution.py:101
  19.5 1.1 copy-start.8
  19.5 351.3 %all-gather.6.cloned.1.call-start = ((), (), s32[]{:S(2)}) async-start(), calls=%async_computation.2 | async-start | bytes 20054016 | tf_op jit(solution)/shard_map/all_gather | solution.py:106
  20.1 789.2 %reduce-scatter.5.cloned.1.call-start = ((), (), s32[]{:S(2)}) async-start(), calls=%async_computation.8 | async-start | bytes 417792 | tf_op jit(solution)/shard_map/reduce_scatter | solution.py:167
  153.1 217.7 %copy-start.3 = (bf16[128,256]{1,0:T(8,128)(2,1)S(1)}, bf16[128,256]{1,0:T(8,128)(2,1)}, u32[]{:S(2)}) copy-start(bf16[128,256]{1,0:T(8,128)(2,1)} %param.21) | copy-start | bytes 196612
  619.7 0.7 copy-start.10
  675.5 0.8 copy-start.7
  675.9 1.3 copy-start.4
  675.9 1.3 copy-start.11
  677.1 3.6 copy-start.12
  750.0 124.2 %reduce-scatter.3.cloned.1.call-start = ((), (), s32[]{:S(2)}) async-start(), calls=%async_computation.7 | async-start | bytes 2506752 | tf_op jit(solution)/shard_map/reduce_scatter | solution.py:164
  762.7 113.9 %copy-start.1 = (bf16[768,2304]{1,0:T(8,128)(2,1)S(1)}, bf16[768,2304]{1,0:T(8,128)(2,1)}, u32[]{:S(2)}) copy-start(bf16[768,2304]{1,0:T(8,128)(2,1)} %param.26) | copy-start | bytes 10616836
Sparse Core Ops, SparseCore 0:
  11.8 50.0 all-gather.13
  64.7 46.9 all-gather.9
  113.5 35.0 all-gather.11
  151.3 117.7 all-gather.7
  270.7 100.0 all-gather.5
  750.1 59.1 reduce-scatter.4
  811.8 62.2 reduce-scatter.2
where the time goes:
time: 891 us; the launch traced here: 883 us
  waiting for transfers between devices  429 us (48%)
  other arithmetic  170 us (19%)
  local copies, waits for them, and re-layouts  122 us (14%)
  matrix products  95 us (11%)
  blocking collectives  51.3 us (6%)
  between operations  14.5 us (2%)
    all_gather x1, waiting for transfers between devices, shards(): lax.all_gather(right_own, 'row', axis=0, tiled=True)  116 us
    all_gather x1, waiting for transfers between devices, shards(): lax.all_gather(pair_state, 'col', axis=0, tiled=True)  88.7 us
    dynamic_update_slice x32, other arithmetic, rows_blocks(): normed_groups, left_groups = lax.map(one_group, grouped)  87.3 us
    reduce_scatter x1, waiting for transfers between devices, shards(): lax.psum_scatter(summed.astype(jnp.bfloat16), 'col', scatter_dimension=1,...  60.8 us
    dot_general x17, matrix products, gated_branch(): jnp.einsum('ikc,ce->ike', normed, weight, preferred_element_type=jnp.floa...  57.6 us
    pmax x1, blocking collectives, shards(): lax.pmax(local_max.astype(jnp.bfloat16), 'col').astype(local_max.dtype)  51.3 us
    reduce_scatter x1, waiting for transfers between devices, shards(): lax.psum_scatter(totals.astype(jnp.bfloat16), 'col', scatter_dimension=2,...  44.8 us
    all_gather x1, waiting for transfers between devices, shards(): lax.all_gather(values_own, 'row', axis=1, tiled=True)  44.2 us
  transfers between devices with their start and end apart: 7, of which 7 were waited for; matrix products, arithmetic and copies ran while one was open for 6% of the time, Pallas kernels for 0%

commit v1 on v0

v1 whole, which is shorter than its diff:
```python
import functools
import math

import jax
import jax.numpy as jnp
from jax import lax
from jax.experimental import pallas as pl
from jax.experimental.pallas import tpu as pltpu
from jax.sharding import PartitionSpec as P

epsilon = 1e-05
bf16 = jnp.bfloat16
f32 = jnp.float32
NT = (((1,), (1,)), ((), ()))
TN = (((0,), (0,)), ((), ()))


def norm_lanes(x):
    centered = x - jnp.mean(x, axis=-1, keepdims=True)
    variance = jnp.mean(centered * centered, axis=-1, keepdims=True)
    return centered * lax.rsqrt(variance + epsilon)


def swap01(x):
    return jnp.swapaxes(x, 0, 1)


class Exchange:
    def __init__(self, axis, size, source, target, landing, send_sem, recv_sem, local_sem):
        self.axis = axis
        self.size = size
        self.source = source
        self.target = target
        self.landing = landing
        self.send_sem = send_sem
        self.recv_sem = recv_sem
        self.local_sem = local_sem

    def me(self):
        return lax.axis_index(self.axis)

    def peer(self, step):
        return lax.rem(self.me() + step, self.size)

    def own(self):
        return pltpu.make_async_copy(
            self.source(self.me()), self.target(self.me()), self.local_sem
        )

    def copy(self, peer, sender):
        return pltpu.make_async_remote_copy(
            src_ref=self.source(peer),
            dst_ref=self.target(sender),
            send_sem=self.send_sem.at[peer],
            recv_sem=self.recv_sem.at[sender],
            device_id={self.axis: peer},
            device_id_type=pl.DeviceIdType.MESH,
        )

    def start(self):
        def step(p, carry):
            self.copy(self.peer(p), self.me()).start()
            return carry

        lax.fori_loop(1, self.size, step, 0)
        self.own().start()

    def wait_recv(self):
        self.own().wait()

        def step(p, carry):
            other = self.peer(p)
            self.copy(other, other).wait_recv()
            return carry

        lax.fori_loop(1, self.size, step, 0)

    def wait_send(self):
        def step(p, carry):
            other = self.peer(p)
            self.copy(other, other).wait_send()
            return carry

        lax.fori_loop(1, self.size, step, 0)


def kernel(
    rows,
    cols,
    pair_ref,
    single_ref,
    valid_ref,
    forbid_ref,
    pair_gain_ref,
    mix_gain_ref,
    left_ref,
    right_ref,
    gate_ref,
    out_w_ref,
    bias_ref,
    token_ref,
    merge_ref,
    tiles_out,
    attn_out,
    wt,
    send_a,
    recv_a,
    send_b,
    recv_l,
    recv_r,
    send_c,
    recv_c,
    send_d,
    recv_d,
    row_f,
    send_p,
    recv_p,
    pair_j,
    gate_j,
    proj,
    send_q,
    recv_q,
    query,
    send_k,
    recv_k,
    bias_j,
    send_e,
    recv_e,
    bias_t,
    bias_s,
    att,
    send_f,
    recv_f,
    *sems,
):
    flat = pair_ref.shape[0]
    tokens = pair_ref.shape[1]
    channels = pair_ref.shape[2]
    samples = single_ref.shape[0] // flat
    width = single_ref.shape[1]
    heads = cols
    head = width // heads
    block = flat * cols
    sem_iter = iter(sems)

    def exchange(axis, size, source, target):
        return Exchange(
            axis, size, source, target, None, next(sem_iter), next(sem_iter), next(sem_iter)
        )

    row = lax.axis_index("row")
    col = lax.axis_index("col")
    own = (row * cols + col) * flat

    ch8 = channels // cols
    ex_a = exchange(
        "col",
        cols,
        lambda p: send_a.at[:, :, pl.ds(pl.multiple_of(p * ch8, ch8), ch8), :],
        lambda s: recv_a.at[s],
    )
    ex_p = exchange("col", cols, lambda p: send_p.at[p], lambda s: recv_p.at[s])
    ex_q = exchange("col", cols, lambda p: send_q.at[p], lambda s: recv_q.at[s])
    ex_l = exchange(
        "row", rows, lambda p: send_b.at[p, 0], lambda s: recv_l.at[s, pl.ds(0, block)]
    )
    ex_r = exchange("row", rows, lambda p: send_b.at[p, 1], lambda s: recv_r.at[s])
    ex_k = exchange("row", rows, lambda p: send_k, lambda s: recv_k.at[s])
    ex_c = exchange("row", rows, lambda p: send_c.at[p], lambda s: recv_c.at[s])
    ex_d = exchange(
        "col",
        cols,
        lambda p: send_d.at[p],
        lambda s: recv_d.at[:, pl.ds(pl.multiple_of(s * ch8, ch8), ch8), :],
    )
    ex_e = exchange("col", cols, lambda p: send_e.at[p], lambda s: recv_e.at[s])
    ex_f = exchange("col", cols, lambda p: send_f.at[p], lambda s: recv_f.at[s])

    barrier = pltpu.get_barrier_semaphore()

    def greet(axis, size):
        def step(p, carry):
            peer = lax.rem(lax.axis_index(axis) + p, size)
            pl.semaphore_signal(
                barrier, inc=1, device_id={axis: peer}, device_id_type=pl.DeviceIdType.MESH
            )
            return carry

        lax.fori_loop(1, size, step, 0)

    greet("col", cols)
    greet("row", rows)

    two = 2 * channels
    wt[0:two, :] = left_ref[...].astype(f32).T.astype(bf16)
    wt[two : 2 * two, :] = right_ref[...].astype(f32).T.astype(bf16)
    token_lane = lax.broadcasted_iota(jnp.int32, (1, tokens), 1)
    gain = pair_gain_ref[...]
    chunk = 256

    def project(t, carry):
        valid = valid_ref[...]
        valid_own = jnp.sum(jnp.where(token_lane == own + t, valid, 0.0), axis=1, keepdims=True)
        for start in range(0, tokens, chunk):
            x = pair_ref[t, start : start + chunk, :].astype(f32)
            normed = (norm_lanes(x) * gain).astype(bf16)
            mask = valid[:, start : start + chunk] * valid_own
            for side in range(2):
                hidden = lax.dot_general(
                    wt[side * two : (side + 1) * two, :], normed, NT, preferred_element_type=f32
                )
                gated = jax.nn.sigmoid(hidden[:channels]) * hidden[channels:] * mask
                send_a[t, side, :, start : start + chunk] = gated.astype(bf16)
        return carry

    lax.fori_loop(0, flat, project, 0)
    pl.semaphore_wait(barrier, cols - 1 + rows - 1)
    ex_a.start()

    def pair_rows(t, carry):
        row_f[0:tokens, :] = pair_ref[t].astype(f32)

        def piece(n, inner):
            a = n // cols
            c = lax.rem(n, cols)
            send_p[c, t, a] = row_f[pl.ds(n * flat, 8), :].astype(bf16)
            return inner

        lax.fori_loop(0, rows * cols, piece, 0, unroll=8)
        return carry

    row_f[tokens : tokens + 8, :] = jnp.zeros((8, channels), f32)
    lax.fori_loop(0, flat, pair_rows, 0)
    ex_p.start()

    own_rows = flat * samples
    proj[...] = (
        jnp.dot(single_ref[...], token_ref[...], preferred_element_type=f32)
        .astype(bf16)
        .astype(f32)
    )
    lane = lax.broadcasted_iota(jnp.int32, (own_rows, 128), 1)

    def window(start, at):
        base = start // 128 * 128
        offset = start - base
        size = 128 if offset + head <= 128 else 256
        x = proj[:, base : base + size]
        shift = (at - offset) % size
        if shift:
            x = pltpu.roll(x, shift, 1)
        return x[:, :128]

    first = lane < head
    second = (lane >= head) & (lane < 2 * head)
    ones = jnp.where(lane == 2 * head, 1.0, 0.0)
    for h in range(heads):
        q = window(h * head, head)
        k = window(width + h * head, head)
        v = window(2 * width + h * head, 0)
        send_q[h, :, 0:128] = jnp.where(second, q, 0.0).astype(bf16)
        send_q[h, :, 128:256] = jnp.where(first, v, jnp.where(second, k, ones)).astype(bf16)
    ex_q.start()

    recv_l[:, block:128, :] = jnp.zeros((rows, 128 - block, tokens), bf16)
    ex_a.wait_recv()

    def to_channels(t, carry):
        at = pl.ds(pl.multiple_of(t * cols, cols), cols)
        for side in range(2):
            send_b[:, side, at, :] = swap01(recv_a[:, t, side])
        return carry

    lax.fori_loop(0, flat, to_channels, 0)
    ex_l.start()
    ex_r.start()

    ex_q.wait_recv()

    def to_samples(t, carry):
        at = pl.ds(pl.multiple_of(t * samples, samples), samples)
        put = pl.ds(pl.multiple_of(t * cols, cols), cols)
        x = swap01(recv_q[:, at, :])
        query[:, put, :] = x[:, :, 0:128]
        send_k[:, put, :] = x[:, :, 128:256]
        return carry

    lax.fori_loop(0, flat, to_samples, 0)
    ex_k.start()

    ex_p.wait_recv()

    def pair_columns(n, carry):
        a = n // flat
        t = lax.rem(n, flat)
        put = pl.ds(pl.multiple_of(t * cols, cols), cols)
        pair_j[a, :, put, :] = swap01(recv_p[:, t, a])
        return carry

    lax.fori_loop(0, rows * flat, pair_columns, 0)

    def gates(n, carry):
        a = n // flat
        t = lax.rem(n, flat)
        normed = (norm_lanes(pair_j[a, t].astype(f32)) * gain).astype(bf16)
        gate_j[n] = jax.nn.sigmoid(jnp.dot(normed, gate_ref[...], preferred_element_type=f32))
        return carry

    lax.fori_loop(0, rows * flat, gates, 0)

    ex_l.wait_recv()
    ex_r.wait_recv()
    part = tokens // 3

    def triangle(n, carry):
        lhs = recv_l[pl.ds(n * 2, 2)].reshape(256, tokens)
        for piece in range(3):
            rhs = recv_r[...].reshape(tokens, tokens)[piece * part : (piece + 1) * part]
            mixed = lax.dot_general(rhs, lhs, NT, preferred_element_type=f32).astype(bf16)
            send_c[n * 2, piece * part : (piece + 1) * part, :] = mixed[:, 0:128]
            send_c[n * 2 + 1, piece * part : (piece + 1) * part, :] = mixed[:, 128:256]
        return carry

    lax.fori_loop(0, rows // 2, triangle, 0)
    ex_c.start()
    ex_c.wait_recv()

    def to_pairs(n, carry):
        at = pl.ds(pl.multiple_of(n * cols, cols), cols)
        send_d[:, n] = swap01(recv_c[:, at, :])
        return carry

    lax.fori_loop(0, rows * flat, to_pairs, 0)
    ex_d.start()
    ex_d.wait_recv()

    mix_gain = mix_gain_ref[...]
    bias_w = bias_ref[...].astype(f32).T.astype(bf16)

    def update_columns(a, carry):
        new = []
        for t in range(flat):
            n = a * flat + t
            mixed = recv_d[n].astype(f32)
            centered = mixed - jnp.mean(mixed, axis=0, keepdims=True)
            variance = jnp.mean(centered * centered, axis=0, keepdims=True)
            mixed_norm = (centered * lax.rsqrt(variance + epsilon) * mix_gain).astype(bf16)
            update = lax.dot_general(mixed_norm, out_w_ref[...], TN, preferred_element_type=f32)
            pair_new = pair_j[a, t].astype(f32) + gate_j[n] * update[:block]
            pair_new = pair_new.astype(bf16).astype(f32)
            new.append(pair_new)
            bias_input = norm_lanes(pair_new).astype(bf16)
            bias_j[a, t, :, 0:block] = lax.dot_general(
                bias_w, bias_input, NT, preferred_element_type=f32
            )
        zero = jnp.zeros((block, channels), f32)
        stacked = swap01(jnp.stack(new + [zero] * (8 - flat), axis=0))
        for t in range(flat):
            tile = stacked[t * cols : (t + 1) * cols, 0:flat, :]
            tiles_out[:, t, a] = tile.astype(bf16)
        send_e[:, a] = swap01(bias_j[a])
        return carry

    bias_j[...] = jnp.zeros(bias_j.shape, f32)
    lax.fori_loop(0, rows, update_columns, 0)
    ex_e.start()
    ex_e.wait_recv()

    for a in range(rows):
        x = swap01(recv_e[:, a])
        bias_t[a * block : (a + 1) * block, :] = x[0:flat].reshape(block, 128)
    for n in range(tokens // 128):
        at = slice(n * 128, (n + 1) * 128)
        bias_s[:, at] = bias_t[at, :].T[0:block] + forbid_ref[:, at]
    ex_k.wait_recv()
    score_scale = 1.0 / math.sqrt(head)

    def attend(s, carry):
        keys = recv_k[:, s].reshape(tokens, 128)
        scores = lax.dot_general(query[s], keys, NT, preferred_element_type=f32)
        scores = scores * score_scale + bias_s[...]
        row_max = jnp.max(scores, axis=-1, keepdims=True)
        weights = jnp.exp(scores - row_max).astype(bf16)
        summed = jnp.dot(weights, keys, preferred_element_type=f32)
        att[s] = (summed / summed[:, 2 * head : 2 * head + 1]).astype(bf16)
        return carry

    lax.fori_loop(0, samples, attend, 0)

    def to_tokens(t, carry):
        at = pl.ds(pl.multiple_of(t * cols, cols), cols)
        put = pl.ds(pl.multiple_of(t * samples, samples), samples)
        send_f[:, put, :] = swap01(att[:, at, :])
        return carry

    lax.fori_loop(0, flat, to_tokens, 0)
    ex_f.start()
    ex_f.wait_recv()
    merged = jnp.zeros((own_rows, width), f32)
    for h in range(heads):
        merged = merged + jnp.dot(
            recv_f[h][:, :head],
            merge_ref[h * head : (h + 1) * head, :],
            preferred_element_type=f32,
        )
    attn_out[...] = swap01(merged.reshape(flat, samples, width)).astype(bf16)

    for ex in (ex_a, ex_p, ex_q, ex_l, ex_r, ex_k, ex_c, ex_d, ex_e, ex_f):
        ex.wait_send()


def shards(
    pair_state,
    single_rep,
    token_mask,
    chain_ids,
    pair_gain,
    mix_gain,
    left_weight,
    right_weight,
    gate_weight,
    out_weight,
    bias_weight,
    token_weight,
    merge_weight,
):
    rows = lax.axis_size("row")
    cols = lax.axis_size("col")
    row_index = lax.axis_index("row")
    flat, tokens, channels = pair_state.shape
    samples, _, width = single_rep.shape
    heads = bias_weight.shape[1]
    block = flat * cols

    def key_order(x):
        return x.reshape(rows, cols, flat).transpose(0, 2, 1)

    ids = key_order(jnp.arange(tokens, dtype=jnp.int32))
    chains = key_order(chain_ids)
    valid = token_mask == 1
    ids_rows = lax.dynamic_index_in_dim(ids, row_index, 0, False).reshape(block)
    chain_rows = lax.dynamic_index_in_dim(chains, row_index, 0, False).reshape(block)
    allowed = key_order(valid).reshape(1, tokens) & (
        chain_rows[:, None] == chains.reshape(1, tokens)
    ) | (ids_rows[:, None] == ids.reshape(1, tokens))
    forbid = jnp.where(allowed, 0.0, -1e30).astype(f32)
    single_rows = single_rep.transpose(1, 0, 2).reshape(flat * samples, width)

    def vmem(*shape, dtype=bf16):
        return pltpu.VMEM(shape, dtype)

    own_rows = flat * samples
    ch8 = channels // cols
    pieces = rows * flat
    scratch = [
        vmem(4 * channels, channels),
        vmem(flat, 2, channels, tokens),
        vmem(cols, flat, 2, ch8, tokens),
        vmem(ch8, 2, block, tokens),
        vmem(rows, 128, tokens),
        vmem(rows, block, tokens),
        vmem(rows, tokens, 128),
        vmem(rows, tokens, 128),
        vmem(cols, pieces, ch8, 128),
        vmem(pieces, channels, 128),
        vmem(tokens + 8, channels, dtype=f32),
        vmem(cols, flat, rows, 8, channels),
        vmem(cols, flat, rows, 8, channels),
        vmem(rows, 8, block, channels),
        vmem(pieces, block, channels, dtype=f32),
        vmem(own_rows, 3 * width, dtype=f32),
        vmem(cols, own_rows, 256),
        vmem(cols, own_rows, 256),
        vmem(samples, block, 128),
        vmem(samples, block, 128),
        vmem(rows, samples, block, 128),
        vmem(rows, 8, heads, 128, dtype=f32),
        vmem(cols, rows, 8, 128, dtype=f32),
        vmem(cols, rows, 8, 128, dtype=f32),
        vmem(tokens, 128, dtype=f32),
        vmem(block, tokens, dtype=f32),
        vmem(samples, block, 128),
        vmem(cols, own_rows, 128),
        vmem(cols, own_rows, 128),
    ]
    for size in (cols, cols, cols, rows, rows, rows, rows, cols, cols, cols):
        scratch += [
            pltpu.SemaphoreType.DMA((size,)),
            pltpu.SemaphoreType.DMA((size,)),
            pltpu.SemaphoreType.DMA,
        ]
    whole = pl.BlockSpec(memory_space=pltpu.VMEM)
    tiles, attention_out = pl.pallas_call(
        functools.partial(kernel, rows, cols),
        out_shape=(
            jax.ShapeDtypeStruct((cols, flat, rows, flat, channels), bf16),
            jax.ShapeDtypeStruct((samples, flat, width), bf16),
        ),
        in_specs=[whole] * 13,
        out_specs=(whole, whole),
        scratch_shapes=scratch,
        compiler_params=pltpu.CompilerParams(
            collective_id=0, has_side_effects=True, vmem_limit_bytes=60 * 1024 * 1024
        ),
    )(
        pair_state,
        single_rows,
        valid.astype(f32).reshape(1, tokens),
        forbid,
        pair_gain.reshape(1, channels),
        mix_gain.reshape(channels, 1),
        left_weight,
        right_weight,
        gate_weight,
        out_weight,
        bias_weight,
        token_weight,
        merge_weight,
    )
    return tiles.reshape(block, rows, 1, flat, channels), attention_out


def solution(mesh):
    in_specs = (
        P(("row", "col"), None, None),
        P(None, ("row", "col"), None),
        P(),
        P(),
        P(),
        P(),
        P(),
        P(),
        P(),
        P(),
        P(),
        P(),
        P(),
    )
    out_specs = (P("row", None, "col", None, None), P(None, ("row", "col"), None))
    return jax.shard_map(shards, mesh=mesh, in_specs=in_specs, out_specs=out_specs, check_vma=False)
```

time: 891 us -> 241 us (0.27)
  waiting for transfers between devices: 429 us -> 0 us
  Pallas kernels: 0 us -> 231 us
  other arithmetic: 170 us -> 1.57 us
  local copies, waits for them, and re-layouts: 122 us -> 8.47 us
  matrix products: 95 us -> 0 us
  blocking collectives: 51.3 us -> 0 us
  between operations: 14.5 us -> 0.69 us
    all_gather x5 -> x0, waiting for transfers between devices: 322 us -> none  [the longest x1 116 us: shards(): lax.all_gather(right_own, 'row', axis=0, tiled=True)]
    pallas_call x0 -> x1, Pallas kernels: none -> 231 us  [shards(): pl.pallas_call(functools.partial(kernel, rows, cols), out_shape=(jax.Shap...]
    reduce_scatter x2 -> x0, waiting for transfers between devices: 106 us -> none  [the longest x1 60.8 us: shards(): lax.psum_scatter(summed.astype(jnp.bfloat16), 'col', scatter_dimension=1,...]
    dot_general x25 -> x0, matrix products: 95 us -> none  [the longest x17 57.6 us: gated_branch(): jnp.einsum('ikc,ce->ike', normed, weight, preferred_element_type=jnp.floa...]
    dynamic_update_slice x32 -> x0, other arithmetic: 87.3 us -> none  [rows_blocks(): normed_groups, left_groups = lax.map(one_group, grouped)]
    reduce_sum x37 -> x0, other arithmetic: 76.3 us -> none  [the longest x19 43.2 us: normalize(): variance = jnp.mean(centered * centered, axis=-1, keepdims=True)]
    pmax x1 -> x0, blocking collectives: 51.3 us -> none  [shards(): lax.pmax(local_max.astype(jnp.bfloat16), 'col').astype(local_max.dtype)]
    all_gather x4 -> x0, local copies, waits for them, and re-layouts: 38.5 us -> none  [the longest x1 16.7 us: shards(): lax.all_gather(pair_state, 'col', axis=0, tiled=True)]
  transfers between devices with their start and end apart: 7 -> 0, of which waited for: 7 -> 0; matrix products, arithmetic and copies ran while one was open for 6% -> 0% of each run, Pallas kernels for 0% -> 0%
where the time goes in v1:
time: 241 us
  Pallas kernels  231 us (96%)
  local copies, waits for them, and re-layouts  8.47 us (4%)
    pallas_call x1, Pallas kernels, shards(): pl.pallas_call(functools.partial(kernel, rows, cols), out_shape=(jax.Shap...  231 us

profile of v1, /device:TPU:1, one launch (start us, length us, event | category | flops | bytes accessed | tf_op | source)
XLA Modules:
  0.0 241.3 jit_solution(11935441190957276362)
XLA Ops:
  0.6 0.1 eq.45
  0.7 0.7 fusion.2
  1.4 0.6 reshape.113.valid_ref
  2.0 0.2 reshape.94
  2.2 0.1 copy.19
  2.3 0.1 and.11
  2.4 1.4 copy.23.bias_ref
  3.8 0.1 reshape.108
  3.9 0.8 reshape.95
  4.7 0.1 copy.20
  4.8 0.1 eq.40
  4.9 0.1 copy.21
  5.0 0.1 eq.42
  5.1 1.4 copy.22.mix_gain_ref
  6.5 0.9 or_select_fusion.forbid_ref
  7.3 230.5 %shard_map.140 = (bf16[16,6,8,6,128]{4,3,2,1,0:T(8,128)(2,1)}, bf16[16,6,768]{2,1,0:T(8,128)(2,1)}) custom-call(bf16[6,768,128]{2,1,0:T(8,128)(2,1)} %pair_ref.1, bf16[96,768]{1,0:T(8,128)(2,1)} %bitcast.14, f32[1,768]{1,0:T(1,128)} %reshape.113.valid_ref, f32[96,768]{1,0:T(8,128)} %or_select_fusion.forbid_ref, f32[1,128]{1,0:T(1,128)} %bitcast.17, ...), custom_call_target="tpu_custom_call" | custom-call | tf_op jit(solution)/shard_map/pallas_call | solution.py:493
  237.9 0.0 copy-start
  237.9 2.7 %copy.24 = bf16[96,8,1,6,128]{4,1,3,2,0:T(8,128)(2,1)} copy(bf16[96,8,1,6,128]{4,3,1,0,2:T(8,128)(2,1)} %bitcast.12) | data formatting | bytes 2359296
  240.6 0.0 copy-done
  240.6 0.7 copy.25
  (3 shorter events, 0.0 us)
Async XLA Ops:
  237.9 2.7 %copy-start = (bf16[16,6,768]{2,1,0:T(8,128)(2,1)S(1)}, bf16[16,6,768]{2,1,0:T(8,128)(2,1)}, u32[]{:S(2)}) copy-start(bf16[16,6,768]{2,1,0:T(8,128)(2,1)} %get-tuple-element.9) | copy-start | bytes 442372

commit v2 on v1

v2 whole, which is shorter than its diff:
```python
import functools
import math

import jax
import jax.numpy as jnp
from jax import lax
from jax.experimental import pallas as pl
from jax.experimental.pallas import tpu as pltpu
from jax.sharding import PartitionSpec as P

epsilon = 1e-05
bf16 = jnp.bfloat16
f32 = jnp.float32
NT = (((1,), (1,)), ((), ()))
TN = (((0,), (0,)), ((), ()))


def norm_lanes(x):
    centered = x - jnp.mean(x, axis=-1, keepdims=True)
    variance = jnp.mean(centered * centered, axis=-1, keepdims=True)
    return centered * lax.rsqrt(variance + epsilon)


def swap01(x):
    return jnp.swapaxes(x, 0, 1)


def pair_groups(rows):
    return max(1, rows // 2)


class Exchange:
    def __init__(self, axis, size, chunks, source, target, sems):
        self.axis = axis
        self.size = size
        self.chunks = chunks
        self.source = source
        self.target = target
        self.send_sem, self.recv_sem, self.local_sem = sems

    def me(self):
        return lax.axis_index(self.axis)

    def own(self, chunk):
        return pltpu.make_async_copy(
            self.source(self.me(), chunk), self.target(self.me(), chunk), self.local_sem.at[chunk]
        )

    def copy(self, peer, sender, chunk):
        return pltpu.make_async_remote_copy(
            src_ref=self.source(peer, chunk),
            dst_ref=self.target(sender, chunk),
            send_sem=self.send_sem.at[chunk, peer],
            recv_sem=self.recv_sem.at[chunk, sender],
            device_id={self.axis: peer},
            device_id_type=pl.DeviceIdType.MESH,
        )

    def each(self, act):
        def step(p, carry):
            act(lax.rem(self.me() + p, self.size))
            return carry

        lax.fori_loop(1, self.size, step, 0)

    def start(self, chunk=0):
        self.each(lambda other: self.copy(other, self.me(), chunk).start())
        self.own(chunk).start()

    def wait_recv(self, chunk=0):
        self.own(chunk).wait()
        self.each(lambda other: self.copy(other, other, chunk).wait_recv())

    def wait_send(self):
        def step(chunk, carry):
            self.each(lambda other: self.copy(other, other, chunk).wait_send())
            return carry

        lax.fori_loop(0, self.chunks, step, 0)


def kernel(
    rows,
    cols,
    pair_ref,
    single_ref,
    valid_ref,
    forbid_ref,
    pair_gain_ref,
    mix_gain_ref,
    left_ref,
    right_ref,
    gate_ref,
    out_w_ref,
    bias_ref,
    token_ref,
    merge_ref,
    tiles_out,
    attn_out,
    wt,
    send_a,
    recv_a,
    send_b,
    recv_l,
    recv_r,
    send_c,
    recv_c,
    send_d,
    recv_d,
    row_f,
    send_p,
    recv_p,
    pair_j,
    gate_j,
    proj,
    send_q,
    recv_q,
    query,
    send_k,
    recv_k,
    bias_j,
    send_e,
    recv_e,
    bias_t,
    bias_s,
    att,
    send_f,
    recv_f,
    *sems,
):
    flat = pair_ref.shape[0]
    tokens = pair_ref.shape[1]
    channels = pair_ref.shape[2]
    samples = single_ref.shape[0] // flat
    width = single_ref.shape[1]
    heads = cols
    head = width // heads
    block = flat * cols
    mixes = pair_groups(rows)
    group = rows // mixes
    sem_iter = iter(sems)

    def exchange(axis, size, chunks, source, target):
        three = next(sem_iter), next(sem_iter), next(sem_iter)
        return Exchange(axis, size, chunks, source, target, three)

    row = lax.axis_index("row")
    col = lax.axis_index("col")
    own = (row * cols + col) * flat
    ch8 = channels // cols

    def tile(p):
        return pl.ds(pl.multiple_of(p * ch8, ch8), ch8)

    def span(n, size):
        return pl.ds(pl.multiple_of(n * size, size), size)

    ex_a = exchange(
        "col", cols, flat, lambda p, t: send_a.at[t, :, tile(p), :], lambda s, t: recv_a.at[s, t]
    )
    ex_p = exchange("col", cols, 1, lambda p, _: send_p.at[p], lambda s, _: recv_p.at[s])
    ex_q = exchange("col", cols, 1, lambda p, _: send_q.at[p], lambda s, _: recv_q.at[s])
    ex_l = exchange(
        "row",
        rows,
        flat,
        lambda p, t: send_b.at[p, 0, span(t, cols)],
        lambda s, t: recv_l.at[s, span(t, cols)],
    )
    ex_r = exchange(
        "row",
        rows,
        flat,
        lambda p, t: send_b.at[p, 1, span(t, cols)],
        lambda s, t: recv_r.at[s, span(t, cols)],
    )
    ex_k = exchange("row", rows, 1, lambda p, _: send_k, lambda s, _: recv_k.at[s])
    ex_c = exchange(
        "row",
        rows,
        mixes,
        lambda p, n: send_c.at[p, span(n, group * block)],
        lambda s, n: recv_c.at[s, span(n, group * block)],
    )
    ex_d = exchange(
        "col",
        cols,
        mixes,
        lambda p, n: send_d.at[p, pl.ds(n * group * flat, group * flat)],
        lambda s, n: recv_d.at[pl.ds(n * group * flat, group * flat), tile(s), :],
    )
    ex_e = exchange(
        "col",
        cols,
        mixes,
        lambda p, n: send_e.at[p, pl.ds(n * group, group)],
        lambda s, n: recv_e.at[s, pl.ds(n * group, group)],
    )
    ex_f = exchange("col", cols, 1, lambda p, _: send_f.at[p], lambda s, _: recv_f.at[s])

    barrier = pltpu.get_barrier_semaphore()

    def greet(axis, size):
        def step(p, carry):
            peer = lax.rem(lax.axis_index(axis) + p, size)
            pl.semaphore_signal(
                barrier, inc=1, device_id={axis: peer}, device_id_type=pl.DeviceIdType.MESH
            )
            return carry

        lax.fori_loop(1, size, step, 0)

    two = 2 * channels
    gain = pair_gain_ref[...]
    own_rows = flat * samples

    def project():
        wt[0:two, :] = left_ref[...].astype(f32).T.astype(bf16)
        wt[two : 2 * two, :] = right_ref[...].astype(f32).T.astype(bf16)
        token_lane = lax.broadcasted_iota(jnp.int32, (1, tokens), 1)
        chunk = 256

        def step(t, carry):
            valid = valid_ref[...]
            valid_own = jnp.sum(jnp.where(token_lane == own + t, valid, 0.0), axis=1, keepdims=True)
            for start in range(0, tokens, chunk):
                x = pair_ref[t, start : start + chunk, :].astype(f32)
                normed = (norm_lanes(x) * gain).astype(bf16)
                mask = valid[:, start : start + chunk] * valid_own
                for side in range(2):
                    hidden = lax.dot_general(
                        wt[side * two : (side + 1) * two, :], normed, NT, preferred_element_type=f32
                    )
                    gated = jax.nn.sigmoid(hidden[:channels]) * hidden[channels:] * mask
                    send_a[t, side, :, start : start + chunk] = gated.astype(bf16)
            pl.when(t == 0)(lambda: pl.semaphore_wait(barrier, cols - 1 + rows - 1))
            ex_a.start(t)
            return carry

        lax.fori_loop(0, flat, step, 0)

    def pair_rows():
        row_f[tokens : tokens + 8, :] = jnp.zeros((8, channels), f32)

        def step(t, carry):
            row_f[0:tokens, :] = pair_ref[t].astype(f32)

            def piece(n, inner):
                a = n // cols
                c = lax.rem(n, cols)
                send_p[c, t, a] = row_f[pl.ds(n * flat, 8), :].astype(bf16)
                return inner

            lax.fori_loop(0, rows * cols, piece, 0, unroll=8)
            return carry

        lax.fori_loop(0, flat, step, 0)
        ex_p.start()

    def tokens_in():
        proj[...] = (
            jnp.dot(single_ref[...], token_ref[...], preferred_element_type=f32)
            .astype(bf16)
            .astype(f32)
        )
        lane = lax.broadcasted_iota(jnp.int32, (own_rows, 128), 1)

        def window(start, at):
            base = start // 128 * 128
            offset = start - base
            size = 128 if offset + head <= 128 else 256
            x = proj[:, base : base + size]
            shift = (at - offset) % size
            if shift:
                x = pltpu.roll(x, shift, 1)
            return x[:, :128]

        first = lane < head
        second = (lane >= head) & (lane < 2 * head)
        ones = jnp.where(lane == 2 * head, 1.0, 0.0)
        for h in range(heads):
            q = window(h * head, head)
            k = window(width + h * head, head)
            v = window(2 * width + h * head, 0)
            send_q[h, :, 0:128] = jnp.where(second, q, 0.0).astype(bf16)
            send_q[h, :, 128:256] = jnp.where(first, v, jnp.where(second, k, ones)).astype(bf16)
        ex_q.start()

    def to_channels():
        recv_l[:, block:128, :] = jnp.zeros((rows, 128 - block, tokens), bf16)

        def step(t, carry):
            ex_a.wait_recv(t)
            for side in range(2):
                send_b[:, side, span(t, cols), :] = swap01(recv_a[:, t, side])
            ex_l.start(t)
            ex_r.start(t)
            return carry

        lax.fori_loop(0, flat, step, 0)

    def to_samples():
        ex_q.wait_recv()

        def step(t, carry):
            x = swap01(recv_q[:, span(t, samples), :])
            query[:, span(t, cols), :] = x[:, :, 0:128]
            send_k[:, span(t, cols), :] = x[:, :, 128:256]
            return carry

        lax.fori_loop(0, flat, step, 0)
        ex_k.start()

    def pair_columns():
        ex_p.wait_recv()

        def step(n, carry):
            a = n // flat
            t = lax.rem(n, flat)
            pair_j[a, :, span(t, cols), :] = swap01(recv_p[:, t, a])
            return carry

        lax.fori_loop(0, rows * flat, step, 0)

    def gates():
        def step(n, carry):
            a = n // flat
            t = lax.rem(n, flat)
            normed = (norm_lanes(pair_j[a, t].astype(f32)) * gain).astype(bf16)
            gate_j[n] = jax.nn.sigmoid(jnp.dot(normed, gate_ref[...], preferred_element_type=f32))
            return carry

        lax.fori_loop(0, rows * flat, step, 0)

    def triangle():
        def ready(t, carry):
            ex_l.wait_recv(t)
            ex_r.wait_recv(t)
            return carry

        lax.fori_loop(0, flat, ready, 0)

        def step(n, carry):
            rhs = recv_r[pl.ds(n * group, group)].reshape(group * block, tokens)
            for r in range(0, rows, 2):
                lhs = recv_l[r : r + 2].reshape(256, tokens)
                mixed = lax.dot_general(rhs, lhs, NT, preferred_element_type=f32).astype(bf16)
                send_c[r, span(n, group * block), :] = mixed[:, 0:128]
                send_c[r + 1, span(n, group * block), :] = mixed[:, 128:256]
            ex_c.start(n)
            return carry

        lax.fori_loop(0, mixes, step, 0)

    def to_pairs():
        def step(n, carry):
            ex_c.wait_recv(n)

            def piece(k, inner):
                m = n * group * flat + k
                send_d[:, m] = swap01(recv_c[:, span(m, cols), :])
                return inner

            lax.fori_loop(0, group * flat, piece, 0)
            ex_d.start(n)
            return carry

        lax.fori_loop(0, mixes, step, 0)

    def update():
        mix_gain = mix_gain_ref[...].T
        bias_w = bias_ref[...]
        bias_j[...] = jnp.zeros(bias_j.shape, f32)

        def columns(a):
            new = []
            for t in range(flat):
                n = a * flat + t
                mixed = recv_d[n].astype(f32)
                centered = mixed - jnp.mean(mixed, axis=0, keepdims=True)
                variance = jnp.mean(centered * centered, axis=0, keepdims=True)
                mixed_norm = (centered * lax.rsqrt(variance + epsilon) * mix_gain).astype(bf16)
                change = lax.dot_general(mixed_norm, out_w_ref[...], TN, preferred_element_type=f32)
                pair_new = pair_j[a, t].astype(f32) + gate_j[n] * change[:block]
                pair_new = pair_new.astype(bf16).astype(f32)
                new.append(pair_new)
                bias_input = norm_lanes(pair_new).astype(bf16)
                bias_j[a, t, :, 0:block] = lax.dot_general(
                    bias_w, bias_input, NT, preferred_element_type=f32
                )
            zero = jnp.zeros((block, channels), f32)
            stacked = swap01(jnp.stack(new + [zero] * (8 - flat), axis=0))
            for t in range(flat):
                part = stacked[t * cols : (t + 1) * cols, 0:flat, :]
                tiles_out[:, t, a] = part.astype(bf16)
            send_e[:, a] = swap01(bias_j[a])

        def step(n, carry):
            ex_d.wait_recv(n)

            def one(k, inner):
                columns(n * group + k)
                return inner

            lax.fori_loop(0, group, one, 0)
            ex_e.start(n)
            return carry

        lax.fori_loop(0, mixes, step, 0)

    def biases():
        for n in range(mixes):
            ex_e.wait_recv(n)
        for a in range(rows):
            x = swap01(recv_e[:, a])
            bias_t[a * block : (a + 1) * block, :] = x[0:flat].reshape(block, 128)
        for n in range(tokens // 128):
            at = slice(n * 128, (n + 1) * 128)
            bias_s[:, at] = bias_t[at, :].T[0:block] + forbid_ref[:, at]

    def attend():
        score_scale = 1.0 / math.sqrt(head)

        def step(s, carry):
            keys = recv_k[:, s].reshape(tokens, 128)
            scores = lax.dot_general(query[s], keys, NT, preferred_element_type=f32)
            scores = scores * score_scale + bias_s[...]
            row_max = jnp.max(scores, axis=-1, keepdims=True)
            weights = jnp.exp(scores - row_max).astype(bf16)
            summed = jnp.dot(weights, keys, preferred_element_type=f32)
            att[s] = (summed / summed[:, 2 * head : 2 * head + 1]).astype(bf16)
            return carry

        lax.fori_loop(0, samples, step, 0)

    def to_tokens():
        def step(t, carry):
            send_f[:, span(t, samples), :] = swap01(att[:, span(t, cols), :])
            return carry

        lax.fori_loop(0, flat, step, 0)
        ex_f.start()

    def merge():
        merged = jnp.zeros((own_rows, width), f32)
        for h in range(heads):
            merged = merged + jnp.dot(
                recv_f[h][:, :head],
                merge_ref[h * head : (h + 1) * head, :],
                preferred_element_type=f32,
            )
        attn_out[...] = swap01(merged.reshape(flat, samples, width)).astype(bf16)

    greet("col", cols)
    greet("row", rows)
    project()
    tokens_in()
    pair_rows()
    to_channels()
    to_samples()
    pair_columns()
    gates()
    triangle()
    to_pairs()
    update()
    biases()
    ex_k.wait_recv()
    attend()
    to_tokens()
    ex_f.wait_recv()
    merge()
    for ex in (ex_a, ex_p, ex_q, ex_l, ex_r, ex_k, ex_c, ex_d, ex_e, ex_f):
        ex.wait_send()


def shards(
    pair_state,
    single_rep,
    token_mask,
    chain_ids,
    pair_gain,
    mix_gain,
    left_weight,
    right_weight,
    gate_weight,
    out_weight,
    bias_weight,
    token_weight,
    merge_weight,
):
    rows = lax.axis_size("row")
    cols = lax.axis_size("col")
    row_index = lax.axis_index("row")
    flat, tokens, channels = pair_state.shape
    samples, _, width = single_rep.shape
    heads = bias_weight.shape[1]
    block = flat * cols

    def key_order(x):
        return x.reshape(rows, cols, flat).transpose(0, 2, 1)

    ids = key_order(jnp.arange(tokens, dtype=jnp.int32))
    chains = key_order(chain_ids)
    valid = token_mask == 1
    ids_rows = lax.dynamic_index_in_dim(ids, row_index, 0, False).reshape(block)
    chain_rows = lax.dynamic_index_in_dim(chains, row_index, 0, False).reshape(block)
    allowed = key_order(valid).reshape(1, tokens) & (
        chain_rows[:, None] == chains.reshape(1, tokens)
    ) | (ids_rows[:, None] == ids.reshape(1, tokens))
    forbid = jnp.where(allowed, 0.0, -1e30).astype(f32)
    single_rows = single_rep.transpose(1, 0, 2).reshape(flat * samples, width)

    def vmem(*shape, dtype=bf16):
        return pltpu.VMEM(shape, dtype)

    own_rows = flat * samples
    ch8 = channels // cols
    pieces = rows * flat
    scratch = [
        vmem(4 * channels, channels),
        vmem(flat, 2, channels, tokens),
        vmem(cols, flat, 2, ch8, tokens),
        vmem(ch8, 2, block, tokens),
        vmem(rows, 128, tokens),
        vmem(rows, block, tokens),
        vmem(rows, tokens, 128),
        vmem(rows, tokens, 128),
        vmem(cols, pieces, ch8, 128),
        vmem(pieces, channels, 128),
        vmem(tokens + 8, channels, dtype=f32),
        vmem(cols, flat, rows, 8, channels),
        vmem(cols, flat, rows, 8, channels),
        vmem(rows, 8, block, channels),
        vmem(pieces, block, channels, dtype=f32),
        vmem(own_rows, 3 * width, dtype=f32),
        vmem(cols, own_rows, 256),
        vmem(cols, own_rows, 256),
        vmem(samples, block, 128),
        vmem(samples, block, 128),
        vmem(rows, samples, block, 128),
        vmem(rows, 8, heads, 128, dtype=f32),
        vmem(cols, rows, 8, 128, dtype=f32),
        vmem(cols, rows, 8, 128, dtype=f32),
        vmem(tokens, 128, dtype=f32),
        vmem(block, tokens, dtype=f32),
        vmem(samples, block, 128),
        vmem(cols, own_rows, 128),
        vmem(cols, own_rows, 128),
    ]
    mixes = pair_groups(rows)
    for size, chunks in (
        (cols, flat),
        (cols, 1),
        (cols, 1),
        (rows, flat),
        (rows, flat),
        (rows, 1),
        (rows, mixes),
        (cols, mixes),
        (cols, mixes),
        (cols, 1),
    ):
        scratch += [
            pltpu.SemaphoreType.DMA((chunks, size)),
            pltpu.SemaphoreType.DMA((chunks, size)),
            pltpu.SemaphoreType.DMA((chunks,)),
        ]
    whole = pl.BlockSpec(memory_space=pltpu.VMEM)
    tiles, attention_out = pl.pallas_call(
        functools.partial(kernel, rows, cols),
        out_shape=(
            jax.ShapeDtypeStruct((cols, flat, rows, flat, channels), bf16),
            jax.ShapeDtypeStruct((samples, flat, width), bf16),
        ),
        in_specs=[whole] * 13,
        out_specs=(whole, whole),
        scratch_shapes=scratch,
        compiler_params=pltpu.CompilerParams(
            collective_id=0, has_side_effects=True, vmem_limit_bytes=60 * 1024 * 1024
        ),
    )(
        pair_state,
        single_rows,
        valid.astype(f32).reshape(1, tokens),
        forbid,
        pair_gain.reshape(1, channels),
        mix_gain.reshape(1, channels),
        left_weight,
        right_weight,
        gate_weight,
        out_weight,
        bias_weight.T,
        token_weight,
        merge_weight,
    )
    return tiles.reshape(block, rows, 1, flat, channels), attention_out


def solution(mesh):
    in_specs = (
        P(("row", "col"), None, None),
        P(None, ("row", "col"), None),
        P(),
        P(),
        P(),
        P(),
        P(),
        P(),
        P(),
        P(),
        P(),
        P(),
        P(),
    )
    out_specs = (P("row", None, "col", None, None), P(None, ("row", "col"), None))
    return jax.shard_map(shards, mesh=mesh, in_specs=in_specs, out_specs=out_specs, check_vma=False)
```

time: 241 us -> 222 us (0.921)
  Pallas kernels: 231 us -> 214 us
  local copies, waits for them, and re-layouts: 8.47 us -> 5.66 us
    pallas_call x1, Pallas kernels: 231 us -> 214 us  [shards(): pl.pallas_call(functools.partial(kernel, rows, cols), out_shape=(jax.Shap...]
where the time goes in v2:
time: 222 us; the launch traced here: 221 us
  Pallas kernels  214 us (96%)
  local copies, waits for them, and re-layouts  5.66 us (3%)
    pallas_call x1, Pallas kernels, shards(): pl.pallas_call(functools.partial(kernel, rows, cols), out_shape=(jax.Shap...  214 us

profile of v2, /device:TPU:1, one launch (start us, length us, event | category | flops | bytes accessed | tf_op | source)
XLA Modules:
  0.0 221.5 jit_solution(3242342102695500262)
XLA Ops:
  0.6 0.1 eq.45
  0.7 0.7 fusion.2
  1.4 0.6 reshape.113.valid_ref
  2.0 0.2 reshape.94
  2.2 0.1 copy.17
  2.3 0.1 and.11
  2.4 0.1 reshape.108
  2.5 0.8 reshape.95
  3.3 0.1 copy.18
  3.4 0.1 eq.40
  3.5 0.1 copy.19
  3.6 0.1 eq.42
  3.7 0.9 or_select_fusion.forbid_ref
  4.6 213.6 %shard_map.140 = (bf16[16,6,8,6,128]{4,3,2,1,0:T(8,128)(2,1)}, bf16[16,6,768]{2,1,0:T(8,128)(2,1)}) custom-call(bf16[6,768,128]{2,1,0:T(8,128)(2,1)} %pair_ref.1, bf16[96,768]{1,0:T(8,128)(2,1)} %bitcast.15, f32[1,768]{1,0:T(1,128)} %reshape.113.valid_ref, f32[96,768]{1,0:T(8,128)} %or_select_fusion.forbid_ref, f32[1,128]{1,0:T(1,128)} %bitcast.18, ...), custom_call_target="tpu_custom_call" | custom-call | tf_op jit(solution)/shard_map/pallas_call | solution.py:569
  218.1 0.0 copy-start
  218.1 2.7 %copy.20 = bf16[96,8,1,6,128]{4,1,3,2,0:T(8,128)(2,1)} copy(bf16[96,8,1,6,128]{4,3,1,0,2:T(8,128)(2,1)} %bitcast.13) | data formatting | bytes 2359296
  220.8 0.0 copy-done
  220.8 0.7 copy.21
  (3 shorter events, 0.0 us)
Async XLA Ops:
  218.1 2.7 %copy-start = (bf16[16,6,768]{2,1,0:T(8,128)(2,1)S(1)}, bf16[16,6,768]{2,1,0:T(8,128)(2,1)}, u32[]{:S(2)}) copy-start(bf16[16,6,768]{2,1,0:T(8,128)(2,1)} %get-tuple-element.9) | copy-start | bytes 442372
